TPU v7x, 512 devices: a whole 4x8x8 slice. The times are simulated.
512 devices in a mesh: dp: 32 (over y, x), seq: 16 (over z, core).
Axes of the slice: x: 4, y: 8, z: 8, core: 2. Of those that a mesh axis runs over, the one named last changes fastest.
Arguments:
- queries: bfloat16 [32, 2048, 2048], P('dp', 'seq'), may hold values from -6 to 6
- keys_in: bfloat16 [32, 2048, 2048], P('dp', 'seq'), may hold values from -6 to 6
- values_in: bfloat16 [32, 2048, 2048], P('dp', 'seq'), may hold values from -6 to 6
- grad_out: bfloat16 [32, 2048, 2048], P('dp', 'seq'), may hold values from -6 to 6
- feat_w: bfloat16 [2, 16, 128, 128], replicated, may hold values from -0.5 to 0.5
Outputs:
- grad_queries: bfloat16 [32, 2048, 2048], P('dp', 'seq')
- grad_keys: bfloat16 [32, 2048, 2048], P('dp', 'seq')
- grad_values: bfloat16 [32, 2048, 2048], P('dp', 'seq')
- grad_feat: float32 [4096, 128], P('dp')
All inputs are finite; a program needn't handle non-finite values.
Results may differ from a plain program's by a relative error of at most 0.0064.
Values sent between devices are 32-bit elements; how exact they have to be, the bound alone decides.
A program may use at most 128 MiB of HBM per device.

v0:
```python
import math
import jax
import jax.numpy as jnp
from jax import lax
from jax.sharding import PartitionSpec as P


def carried_in(value, axis, join, neutral, backward):
    count, mine = (lax.axis_size(axis), lax.axis_index(axis))
    pieces = lax.all_gather(value, axis)
    if backward:
        pieces = pieces[::-1]
        mine = count - 1 - mine
    running = jnp.full_like(value, 0) + jnp.asarray(neutral, value.dtype)

    def lap(position, running):
        longer = join(running, pieces[position])
        return jnp.where(position < mine, longer, running)

    return lax.fori_loop(0, count - 1, lap, running)


def add_one(earlier, later):
    return earlier + later


def body(queries, keys_in, values_in, grad_out, feat_w):
    seq_count = lax.axis_size("seq")
    rep_count = lax.axis_size("dp")
    rows = queries.shape[1]
    heads = feat_w.shape[1]
    hsize = feat_w.shape[2]
    scale = 1.0 / math.sqrt(hsize * rows * seq_count)
    gscale = 1.0 / math.sqrt(rows * seq_count * rep_count)
    shape = (rows, heads, hsize)
    q_heads = queries[0].reshape(shape)
    k_heads = keys_in[0].reshape(shape)
    v_heads = values_in[0].reshape(shape)
    g_heads = grad_out[0].reshape(shape)
    f32 = jnp.float32
    bf16 = jnp.bfloat16
    feat_q = jnp.einsum("tha,hab->thb", q_heads, feat_w[0], preferred_element_type=f32).astype(bf16)
    feat_k = jnp.einsum("tha,hab->thb", k_heads, feat_w[1], preferred_element_type=f32).astype(bf16)
    sterm = jnp.einsum("tha,thb->hab", feat_k, v_heads, preferred_element_type=f32)
    gterm = jnp.einsum("tha,thb->hab", feat_q, g_heads, preferred_element_type=f32)
    zeros = jnp.zeros(sterm.shape, f32)
    prefix = carried_in(sterm, "seq", add_one, zeros, False)
    suffix = carried_in(gterm, "seq", add_one, zeros, True)
    causal = jnp.tril(jnp.ones((rows, rows), dtype=bool))
    p_mat = jnp.where(
        causal, scale * jnp.einsum("tha,sha->hts", feat_q, feat_k, preferred_element_type=f32), 0.0
    ).astype(bf16)
    q_mat = jnp.where(
        causal,
        scale * jnp.einsum("tha,sha->hts", g_heads, v_heads, preferred_element_type=f32),
        0.0,
    ).astype(bf16)
    state_b = prefix.astype(bf16)
    grad_b = suffix.astype(bf16)
    d_featq = (
        scale * jnp.einsum("thb,hab->tha", g_heads, state_b, preferred_element_type=f32)
        + jnp.einsum("hts,sha->tha", q_mat, feat_k, preferred_element_type=f32)
    ).astype(bf16)
    d_featk = (
        scale * jnp.einsum("thb,hab->tha", v_heads, grad_b, preferred_element_type=f32)
        + jnp.einsum("hts,tha->sha", q_mat, feat_q, preferred_element_type=f32)
    ).astype(bf16)
    d_values = (
        scale * jnp.einsum("tha,hab->thb", feat_k, grad_b, preferred_element_type=f32)
        + jnp.einsum("hts,thb->shb", p_mat, g_heads, preferred_element_type=f32)
    ).astype(bf16)
    d_queries = jnp.einsum("thb,hab->tha", d_featq, feat_w[0], preferred_element_type=f32).astype(
        bf16
    )
    d_keys = jnp.einsum("thb,hab->tha", d_featk, feat_w[1], preferred_element_type=f32).astype(bf16)
    wgrad_q = jnp.einsum("tha,thb->hab", q_heads, d_featq, preferred_element_type=f32)
    wgrad_k = jnp.einsum("tha,thb->hab", k_heads, d_featk, preferred_element_type=f32)
    local_grad = jnp.stack([wgrad_q, wgrad_k]).reshape(2 * heads * hsize, hsize)
    seq_total = lax.psum(local_grad, "seq")
    owned = lax.psum_scatter(seq_total, "dp", scatter_dimension=0, tiled=True)
    flat = (1, rows, heads * hsize)
    return (d_queries.reshape(flat), d_keys.reshape(flat), d_values.reshape(flat), owned * gscale)


def solution(mesh):
    return jax.shard_map(
        body,
        mesh=mesh,
        in_specs=(
            P("dp", "seq", None),
            P("dp", "seq", None),
            P("dp", "seq", None),
            P("dp", "seq", None),
            P(),
        ),
        out_specs=(P("dp", "seq", None), P("dp", "seq", None), P("dp", "seq", None), P("dp", None)),
        check_vma=False,
    )
```

profile of v0, /device:TPU:1, one launch (start us, length us, event | category | flops | bytes accessed | tf_op | source)
XLA Modules:
  0.0 593.4 jit_solution(17331871863249463423)
XLA Ops:
  7.2 1.3 copy.64
  8.5 1.3 copy.67
  9.9 1.6 fusion.11
  11.5 1.3 fusion.27
  12.8 0.0 all-gather.7.cloned.1.call-start
  12.9 1.3 copy.65
  14.2 1.3 copy.66
  15.5 1.6 fusion.12
  17.1 1.5 fusion.33
  18.6 0.0 reduce-scatter.2.cloned.1.call-start
  18.7 2.4 fusion.5
  21.1 96.6 %all-gather.5.cloned.1.call-done = f32[256,128,128]{2,1,0:T(8,128)} async-done(((f32[16,128,128]{2,1,0:T(8,128)}), f32[256,128,128]{2,1,0:T(8,128)}) %all-gather.5.cloned.1.call-update) | async-done | bytes 16777232 | tf_op jit(solution)/shard_map/all_gather | solution.py:10
  117.7 24.4 %while.28 = (s32[]{:T(128)}, f32[16,128,128]{2,1,0:T(8,128)S(1)}, s32[]{:T(128)}, f32[16,16,128,128]{3,2,1,0:T(8,128)}, s32[]{:T(128)}, /*index=5*/s32[]{:T(128)}) while((s32[]{:T(128)}, f32[16,128,128]{2,1,0:T(8,128)S(1)}, s32[]{:T(128)}, f32[16,16,128,128]{3,2,1,0:T(8,128)}, s32[]{:T(128)}, /*index=5*/s32[]{:T(128)}) %tuple.79), condition=%wide.region_1.2_spmd.clone, body=%wide.region_0.1_spmd.clone.sunk | while | flops 786436 | bytes 3145821 | solution.py:20
  117.7 1.6 add_select_fusion.4
  119.3 1.6 add_select_fusion.4
  120.9 1.6 add_select_fusion.4
  122.6 1.6 add_select_fusion.4
  124.2 1.6 add_select_fusion.4
  125.8 1.6 add_select_fusion.4
  127.4 1.6 add_select_fusion.4
  129.0 1.6 add_select_fusion.4
  130.6 1.7 add_select_fusion.4
  132.4 1.6 add_select_fusion.4
  134.0 1.6 add_select_fusion.4
  135.6 1.6 add_select_fusion.4
  137.2 1.6 add_select_fusion.4
  138.8 1.7 add_select_fusion.4
  140.5 1.6 add_select_fusion.4
  142.1 0.3 convolution_multiply_fusion.4
  142.4 1.5 fusion.10
  144.0 2.5 convolution_bitcast_fusion.2
  146.5 70.1 %all-gather.7.cloned.1.call-done = f32[256,128,128]{2,1,0:T(8,128)} async-done(((f32[16,128,128]{2,1,0:T(8,128)}), f32[256,128,128]{2,1,0:T(8,128)}) %all-gather.7.cloned.1.call-update) | async-done | bytes 16777232 | tf_op jit(solution)/shard_map/all_gather | solution.py:10
  216.6 11.6 %rev.3 = f32[16,16,128,128]{3,2,1,0:T(8,128)} reverse(f32[16,16,128,128]{3,2,1,0:T(8,128)} %bitcast.81), dimensions={0} | reverse | bytes 33554432 | tf_op jit(solution)/shard_map/rev | solution.py:12
  228.3 24.2 %while.29 = (s32[]{:T(128)}, f32[16,128,128]{2,1,0:T(8,128)S(1)}, s32[]{:T(128)}, f32[16,16,128,128]{3,2,1,0:T(8,128)}, s32[]{:T(128)}, /*index=5*/s32[]{:T(128)}) while((s32[]{:T(128)}, f32[16,128,128]{2,1,0:T(8,128)S(1)}, s32[]{:T(128)}, f32[16,16,128,128]{3,2,1,0:T(8,128)}, s32[]{:T(128)}, /*index=5*/s32[]{:T(128)}) %tuple.68), condition=%wide.region_3.4_spmd.clone, body=%wide.region_2.3_spmd.clone.sunk | while | flops 786436 | bytes 3145821 | solution.py:20
  228.3 1.6 add_select_fusion.5
  229.9 1.6 add_select_fusion.5
  231.6 1.6 add_select_fusion.5
  233.2 1.6 add_select_fusion.5
  234.8 1.6 add_select_fusion.5
  236.4 1.6 add_select_fusion.5
  238.0 1.6 add_select_fusion.5
  239.6 1.6 add_select_fusion.5
  241.2 1.6 add_select_fusion.5
  242.9 1.6 add_select_fusion.5
  244.5 1.6 add_select_fusion.5
  246.1 1.6 add_select_fusion.5
  247.7 1.6 add_select_fusion.5
  249.3 1.6 add_select_fusion.5
  250.9 1.6 add_select_fusion.5
  252.5 1.5 convolution_multiply_fusion.2
  254.1 1.3 fusion.9
  255.4 0.8 copy-done.2
  256.2 1.5 convolution_bitcast_fusion.1
  257.7 2.8 pad_maximum_fusion
  260.6 2.1 convolution_convert_fusion.1
  262.7 1.3 fusion.1
  264.0 1.7 fusion.8
  265.7 208.6 %reduce-scatter.2.cloned.1.call-done = f32[128,128]{1,0:T(8,128)} async-done(((f32[4096,128]{1,0:T(8,128)}), f32[128,128]{1,0:T(8,128)}) %reduce-scatter.2.cloned.1.call-update) | async-done | bytes 65552 | tf_op jit(solution)/shard_map/reduce_scatter | solution.py:80
  474.3 1.5 convolution_convert_fusion
  475.8 1.0 copy.54
  476.9 2.0 copy.52
  478.9 1.0 copy.53
  479.9 105.5 %all-reduce.2.cloned.1.call-done = f32[128,128]{1,0:T(8,128)} async-done(((f32[128,128]{1,0:T(8,128)}), f32[128,128]{1,0:T(8,128)}) %all-reduce.2.cloned.1.call-update) | async-done | bytes 65552 | tf_op jit(solution)/shard_map/psum | solution.py:79
  585.4 1.5 broadcast_multiply_fusion
  (20 shorter events, 0.2 us)
Async XLA Ops:
  7.2 110.5 %all-gather.5.cloned.1.call-start = ((), (), s32[]{:S(2)}) async-start(), calls=%async_computation.1 | async-start | bytes 17825792 | tf_op jit(solution)/shard_map/all_gather | solution.py:10
  8.5 4.3 copy-start.3
  9.9 5.6 copy-start.4
  12.8 203.8 %all-gather.7.cloned.1.call-start = ((), (), s32[]{:S(2)}) async-start(), calls=%async_computation.2 | async-start | bytes 17825792 | tf_op jit(solution)/shard_map/all_gather | solution.py:10
  15.5 3.2 copy-start.5
  17.1 1.6 copy-start
  18.6 455.7 %reduce-scatter.2.cloned.1.call-start = ((), (), s32[]{:S(2)}) async-start(), calls=%async_computation.3 | async-start | bytes 2162688 | tf_op jit(solution)/shard_map/reduce_scatter | solution.py:80
  228.3 25.8 %copy-start.1 = (bf16[128,16,128]{0,2,1:T(8,128)(2,1)S(1)}, bf16[128,16,128]{0,2,1:T(8,128)(2,1)}, u32[]{:S(2)}) copy-start(bf16[128,16,128]{0,2,1:T(8,128)(2,1)} %copy-done) | copy-start | bytes 1572868
  255.4 0.8 copy-start.2
  260.5 324.9 %all-reduce.2.cloned.1.call-start = ((), (), s32[]{:S(2)}) async-start(), calls=%async_computation.4 | async-start | bytes 131072 | tf_op jit(solution)/shard_map/psum | solution.py:79
Sparse Core Ops, SparseCore 0:
  12.9 104.7 all-gather.4
  119.8 96.7 all-gather.6
  260.6 213.6 reduce-scatter.1
  476.6 108.7 all-reduce.1
where the time goes:
time: 595 us; the launch traced here: 593 us
  waiting for transfers between devices  481 us (81%)
  other arithmetic  52.2 us (9%)
  matrix products  23.7 us (4%)
  local copies, waits for them, and re-layouts  21.8 us (4%)
  between operations  14 us (2%)
    reduce_scatter x1, waiting for transfers between devices, body(): owned = lax.psum_scatter(seq_total, 'dp', scatter_dimension=0, tiled=True)  209 us
    all_gather x2, waiting for transfers between devices, carried_in(): pieces = lax.all_gather(value, axis)  167 us
    psum x1, waiting for transfers between devices, body(): seq_total = lax.psum(local_grad, 'seq')  105 us
    select_n x30, other arithmetic, lap(): return jnp.where(position < mine, longer, running)  48 us
  transfers between devices with their start and end apart: 4, of which 4 were waited for; matrix products, arithmetic and copies ran while one was open for 8% of the time, Pallas kernels for 0%

commit v1 on v0

--- a/solution.py
+++ b/solution.py
@@ -76,7 +76,8 @@
     wgrad_q = jnp.einsum("tha,thb->hab", q_heads, d_featq, preferred_element_type=f32)
     wgrad_k = jnp.einsum("tha,thb->hab", k_heads, d_featk, preferred_element_type=f32)
     local_grad = jnp.stack([wgrad_q, wgrad_k]).reshape(2 * heads * hsize, hsize)
-    seq_total = lax.psum(local_grad, "seq")
+    right_arr = jax.lax.all_gather(local_grad, "seq")
+    seq_total = jnp.sum(right_arr, 0)
     owned = lax.psum_scatter(seq_total, "dp", scatter_dimension=0, tiled=True)
     flat = (1, rows, heads * hsize)
     return (d_queries.reshape(flat), d_keys.reshape(flat), d_values.reshape(flat), owned * gscale)

time: 595 us -> 678 us (1.14)
  waiting for transfers between devices: 481 us -> 548 us
  other arithmetic: 52.2 us -> 65.3 us
    all_gather x0 -> x1, waiting for transfers between devices: none -> 176 us  [body(): right_arr = jax.lax.all_gather(local_grad, 'seq')]
    psum x1 -> x0, waiting for transfers between devices: 105 us -> none  [body(): seq_total = lax.psum(local_grad, 'seq')]
    reduce_sum x0 -> x1, other arithmetic: none -> 13.1 us  [body(): seq_total = jnp.sum(right_arr, 0)]
  transfers between devices with their start and end apart: 4 -> 4, of which waited for: 4 -> 4; matrix products, arithmetic and copies ran while one was open for 8% -> 7% of each run, Pallas kernels for 0% -> 0%
where the time goes in v1:
time: 678 us; the launch traced here: 672 us
  waiting for transfers between devices  548 us (81%)
  other arithmetic  65.3 us (10%)
  matrix products  22.9 us (3%)
  local copies, waits for them, and re-layouts  20.7 us (3%)
  between operations  14 us (2%)
    reduce_scatter x1, waiting for transfers between devices, body(): owned = lax.psum_scatter(seq_total, 'dp', scatter_dimension=0, tiled=True)  205 us
    all_gather x1, waiting for transfers between devices, body(): right_arr = jax.lax.all_gather(local_grad, 'seq')  176 us
    all_gather x2, waiting for transfers between devices, carried_in(): pieces = lax.all_gather(value, axis)  167 us
    select_n x30, other arithmetic, lap(): return jnp.where(position < mine, longer, running)  48 us
  transfers between devices with their start and end apart: 4, of which 4 were waited for; matrix products, arithmetic and copies ran while one was open for 7% of the time, Pallas kernels for 0%

profile of v1, /device:TPU:1, one launch (start us, length us, event | category | flops | bytes accessed | tf_op | source)
XLA Modules:
  0.0 671.6 jit_solution(12270209045013626273)
XLA Ops:
  7.2 1.3 copy.64
  8.5 1.3 copy.67
  9.9 1.6 fusion.11
  11.5 1.3 fusion.27
  12.8 0.0 all-gather.10.cloned.1.call-start
  12.9 1.3 copy.65
  14.2 1.3 copy.66
  15.5 1.6 fusion.12
  17.1 1.5 fusion.33
  18.8 2.4 fusion.5
  21.1 96.6 %all-gather.8.cloned.1.call-done = f32[256,128,128]{2,1,0:T(8,128)} async-done(((f32[16,128,128]{2,1,0:T(8,128)}), f32[256,128,128]{2,1,0:T(8,128)}) %all-gather.8.cloned.1.call-update) | async-done | bytes 16777232 | tf_op jit(solution)/shard_map/all_gather | solution.py:10
  117.7 24.4 %while.28 = (s32[]{:T(128)}, f32[16,128,128]{2,1,0:T(8,128)S(1)}, s32[]{:T(128)}, f32[16,16,128,128]{3,2,1,0:T(8,128)}, s32[]{:T(128)}, /*index=5*/s32[]{:T(128)}) while((s32[]{:T(128)}, f32[16,128,128]{2,1,0:T(8,128)S(1)}, s32[]{:T(128)}, f32[16,16,128,128]{3,2,1,0:T(8,128)}, s32[]{:T(128)}, /*index=5*/s32[]{:T(128)}) %tuple.79), condition=%wide.region_1.2_spmd.clone, body=%wide.region_0.1_spmd.clone.sunk | while | flops 786436 | bytes 3145821 | solution.py:20
  117.7 1.6 add_select_fusion.4
  119.3 1.6 add_select_fusion.4
  121.0 1.6 add_select_fusion.4
  122.6 1.6 add_select_fusion.4
  124.2 1.6 add_select_fusion.4
  125.8 1.6 add_select_fusion.4
  127.4 1.6 add_select_fusion.4
  129.0 1.6 add_select_fusion.4
  130.6 1.7 add_select_fusion.4
  132.4 1.6 add_select_fusion.4
  134.0 1.6 add_select_fusion.4
  135.6 1.6 add_select_fusion.4
  137.2 1.6 add_select_fusion.4
  138.8 1.7 add_select_fusion.4
  140.6 1.6 add_select_fusion.4
  142.2 0.3 convolution_multiply_fusion.4
  142.5 1.5 fusion.10
  144.0 2.5 convolution_bitcast_fusion.2
  146.5 70.1 %all-gather.10.cloned.1.call-done = f32[256,128,128]{2,1,0:T(8,128)} async-done(((f32[16,128,128]{2,1,0:T(8,128)}), f32[256,128,128]{2,1,0:T(8,128)}) %all-gather.10.cloned.1.call-update) | async-done | bytes 16777232 | tf_op jit(solution)/shard_map/all_gather | solution.py:10
  216.7 11.6 %rev.3 = f32[16,16,128,128]{3,2,1,0:T(8,128)} reverse(f32[16,16,128,128]{3,2,1,0:T(8,128)} %bitcast.81), dimensions={0} | reverse | bytes 33554432 | tf_op jit(solution)/shard_map/rev | solution.py:12
  228.3 24.2 %while.29 = (s32[]{:T(128)}, f32[16,128,128]{2,1,0:T(8,128)S(1)}, s32[]{:T(128)}, f32[16,16,128,128]{3,2,1,0:T(8,128)}, s32[]{:T(128)}, /*index=5*/s32[]{:T(128)}) while((s32[]{:T(128)}, f32[16,128,128]{2,1,0:T(8,128)S(1)}, s32[]{:T(128)}, f32[16,16,128,128]{3,2,1,0:T(8,128)}, s32[]{:T(128)}, /*index=5*/s32[]{:T(128)}) %tuple.68), condition=%wide.region_3.4_spmd.clone, body=%wide.region_2.3_spmd.clone.sunk | while | flops 786436 | bytes 3145821 | solution.py:20
  228.3 1.6 add_select_fusion.5
  230.0 1.6 add_select_fusion.5
  231.6 1.6 add_select_fusion.5
  233.2 1.6 add_select_fusion.5
  234.8 1.6 add_select_fusion.5
  236.4 1.6 add_select_fusion.5
  238.0 1.6 add_select_fusion.5
  239.6 1.6 add_select_fusion.5
  241.3 1.6 add_select_fusion.5
  242.9 1.6 add_select_fusion.5
  244.5 1.6 add_select_fusion.5
  246.1 1.6 add_select_fusion.5
  247.7 1.6 add_select_fusion.5
  249.3 1.6 add_select_fusion.5
  250.9 1.6 add_select_fusion.5
  252.5 1.5 convolution_multiply_fusion.2
  254.1 1.3 fusion.9
  255.4 0.8 copy-done.2
  256.2 1.5 convolution_bitcast_fusion.1
  257.7 2.8 pad_maximum_fusion
  260.6 175.9 %all-gather.6.cloned.1.call-done = f32[16,4096,128]{2,1,0:T(8,128)} async-done(((f32[1,4096,128]{2,1,0:T(8,128)}), f32[16,4096,128]{2,1,0:T(8,128)}) %all-gather.6.cloned.1.call-update) | async-done | bytes 33554448 | tf_op jit(solution)/shard_map/all_gather | solution.py:79
  436.5 13.1 %reduce_sum.9 = f32[4096,128]{1,0:T(8,128)} reduce(f32[16,4096,128]{2,1,0:T(8,128)} %all-gather.6.cloned.1.call-done, f32[]{:T(128)} %constant.58.clone.1), dimensions={0}, to_apply=%region_4.5 | reduce | flops 7864320 | bytes 35651588 | tf_op jit(solution)/shard_map/reduce_sum | solution.py:80
  449.6 1.3 fusion.1
  450.9 1.7 fusion.8
  452.6 1.0 copy.54
  453.6 1.3 convolution_convert_fusion.1
  455.0 1.0 copy.52
  456.0 1.5 convolution_convert_fusion
  457.5 1.0 copy.53
  458.5 205.1 %reduce-scatter.2.cloned.1.call-done = f32[128,128]{1,0:T(8,128)} async-done(((f32[4096,128]{1,0:T(8,128)}), f32[128,128]{1,0:T(8,128)}) %reduce-scatter.2.cloned.1.call-update) | async-done | bytes 65552 | tf_op jit(solution)/shard_map/reduce_scatter | solution.py:81
  663.6 1.5 broadcast_multiply_fusion
  (21 shorter events, 0.2 us)
Async XLA Ops:
  7.2 110.6 %all-gather.8.cloned.1.call-start = ((), (), s32[]{:S(2)}) async-start(), calls=%async_computation.3 | async-start | bytes 17825792 | tf_op jit(solution)/shard_map/all_gather | solution.py:10
  8.5 4.3 copy-start.3
  9.9 5.6 copy-start.4
  12.8 203.8 %all-gather.10.cloned.1.call-start = ((), (), s32[]{:S(2)}) async-start(), calls=%async_computation.4 | async-start | bytes 17825792 | tf_op jit(solution)/shard_map/all_gather | solution.py:10
  15.5 3.2 copy-start.5
  17.1 1.6 copy-start
  18.7 417.8 %all-gather.6.cloned.1.call-start = ((), (), s32[]{:S(2)}) async-start(), calls=%async_computation.1 | async-start | bytes 35651584 | tf_op jit(solution)/shard_map/all_gather | solution.py:79
  228.3 25.8 %copy-start.1 = (bf16[128,16,128]{0,2,1:T(8,128)(2,1)S(1)}, bf16[128,16,128]{0,2,1:T(8,128)(2,1)}, u32[]{:S(2)}) copy-start(bf16[128,16,128]{0,2,1:T(8,128)(2,1)} %copy-done) | copy-start | bytes 1572868
  255.4 0.8 copy-start.2
  260.6 403.0 %reduce-scatter.2.cloned.1.call-start = ((), (), s32[]{:S(2)}) async-start(), calls=%async_computation.2 | async-start | bytes 2162688 | tf_op jit(solution)/shard_map/reduce_scatter | solution.py:81
Sparse Core Ops, SparseCore 0:
  12.9 104.7 all-gather.7
  119.8 96.7 all-gather.9
  260.7 175.7 all-gather.5
  449.7 213.8 reduce-scatter.1
